TPU v7x, 512 devices: a whole 4x8x8 slice. The times are simulated.
512 devices in a mesh: gx: 64 (over y, z_lo, core), gy: 8 (over z_hi, x).
Axes of the slice: x: 4, y: 8, z: 8 (z_hi: 2, z_lo: 4; z = z_hi * 4 + z_lo), core: 2. Of those that a mesh axis runs over, the one named last changes fastest.
Arguments:
- pops: float32 [19, 256, 64, 128], P(None, 'gx', 'gy'), may hold values from 0.005 to 0.5, as said below
- label: int32 [256, 64, 128], P('gx', 'gy'), may hold values from 0 to 2, as said below
- drive: float32 [3, 256, 64, 128], P(None, 'gx', 'gy'), may hold values from -0.3 to 0.3
Outputs:
- momentum: float32 [3, 256, 64, 128], P(None, 'gx', 'gy')
- running: float32 [3, 64, 16, 32], P(None, 'gx', 'gy')
Inputs may be any that keep to these rules, and one draw needn't show every extreme that they name: `pops`: populations near a local equilibrium with density 0.8 to 1.2 and each velocity component within 0.1. `label`: 2 marks walls: every cell with z index 0 or 127, and scattered obstacle cells; elsewhere 1 marks the second solution, 0 the first.
All inputs are finite; a program needn't handle non-finite values.
Results may differ from a plain program's by a relative error of at most 0.0003.
Values sent between devices are 32-bit elements; how exact they have to be, the bound alone decides.
No kernel may reach another device: no remote copies, remote signals or barrier semaphores. Data moves between devices by JAX's collectives and lax.ppermute only.
A program may use at most 64 MiB of HBM per device.

v0:
```python
import math
import jax
import jax.numpy as jnp
from jax import lax
from jax.sharding import PartitionSpec as P

NZ = 128
STEPS = 4
VELOCITY = [
    [0, 0, 0],
    [1, 0, 0],
    [-1, 0, 0],
    [0, 1, 0],
    [0, -1, 0],
    [0, 0, 1],
    [0, 0, -1],
    [1, 1, 0],
    [-1, -1, 0],
    [1, -1, 0],
    [-1, 1, 0],
    [1, 0, 1],
    [-1, 0, -1],
    [1, 0, -1],
    [-1, 0, 1],
    [0, 1, 1],
    [0, -1, -1],
    [0, 1, -1],
    [0, -1, 1],
]
OPPOSITE = [0, 2, 1, 4, 3, 6, 5, 8, 7, 10, 9, 12, 11, 14, 13, 16, 15, 18, 17]
WEIGHTS = [1.0 / 3.0] + [1.0 / 18.0] * 6 + [1.0 / 36.0] * 12
PAIRS = [(0, 0), (1, 1), (2, 2), (0, 1), (0, 2), (1, 2)]
COMPONENT = [[0, 3, 4], [3, 1, 5], [4, 5, 2]]
SLOW_VISCOSITY = 0.0004


def with_halo(cells, sides, width):
    for axis, dim in sides:
        count = lax.axis_size(axis)
        head = lax.slice_in_dim(cells, 0, width, axis=dim)
        tail = lax.slice_in_dim(cells, cells.shape[dim] - width, cells.shape[dim], axis=dim)
        cells = jnp.concatenate(
            [
                lax.ppermute(tail, axis, [(i, (i + 1) % count) for i in range(count)]),
                cells,
                lax.ppermute(head, axis, [((i + 1) % count, i) for i in range(count)]),
            ],
            axis=dim,
        )
    return cells


def collide(pops, label, drive, phase):
    columns = [
        jnp.array([row[axis_id] for row in VELOCITY], jnp.float32).reshape(19, 1, 1, 1)
        for axis_id in range(3)
    ]
    weights = jnp.array(WEIGHTS, jnp.float32).reshape(19, 1, 1, 1)
    density = jnp.sum(pops, axis=0)
    moment = [jnp.sum(columns[axis_id] * pops, axis=0) for axis_id in range(3)]
    speed = [moment[axis_id] / density for axis_id in range(3)]
    along = columns[0] * speed[0] + columns[1] * speed[1] + columns[2] * speed[2]
    square = speed[0] * speed[0] + speed[1] * speed[1] + speed[2] * speed[2]
    balance = weights * density * (1.0 + 3.0 * along + 4.5 * along * along - 1.5 * square)
    second = label == 1
    solid = label == 2
    omega = jnp.where(second, 1.1, 1.6)
    strength = jnp.where(second, 0.6, 1.0) * phase
    push = columns[0] * drive[0] + columns[1] * drive[1] + columns[2] * drive[2]
    relaxed = pops - omega * (pops - balance) + 3.0 * weights * strength * push
    bounced = jnp.stack([pops[other] for other in OPPOSITE])
    post = jnp.where(solid, bounced, relaxed)
    fluid = jnp.where(solid, 0.0, 1.0)
    stress = jnp.stack([moment[first] * moment[later] / density * fluid for first, later in PAIRS])
    return (post, stress)


def momentum_of(pops):
    columns = [
        jnp.array([row[axis_id] for row in VELOCITY], jnp.float32).reshape(19, 1, 1, 1)
        for axis_id in range(3)
    ]
    return jnp.stack([jnp.sum(columns[axis_id] * pops, axis=0) for axis_id in range(3)])


def tables(length):
    index = jnp.arange(length, dtype=jnp.int32)
    turns = index[:, None] * index[None, :] % length
    angle = turns.astype(jnp.float32) * (2.0 * math.pi / length)
    return (jnp.cos(angle), jnp.sin(angle))


def product(values, table):
    return jnp.matmul(values, table, precision=lax.Precision.HIGHEST)


def transform(real, imag, axis_id, inverse):
    length = real.shape[axis_id]
    cosine, sine = tables(length)
    real_last = jnp.moveaxis(real, axis_id, -1)
    imag_last = jnp.moveaxis(imag, axis_id, -1)
    if inverse:
        out_real = (product(real_last, cosine) - product(imag_last, sine)) / length
        out_imag = (product(imag_last, cosine) + product(real_last, sine)) / length
    else:
        out_real = product(real_last, cosine) + product(imag_last, sine)
        out_imag = product(imag_last, cosine) - product(real_last, sine)
    return (jnp.moveaxis(out_real, -1, axis_id), jnp.moveaxis(out_imag, -1, axis_id))


def wavenumber(index, length):
    shifted = index - length * (index >= (length + 1) // 2).astype(jnp.int32)
    return shifted.astype(jnp.float32) * (2.0 * math.pi / length)


def local(pops, label, drive):
    width = pops.shape[1]
    height = pops.shape[2]
    state = pops
    total = jnp.zeros((6,) + pops.shape[1:], jnp.float32)
    for step in range(STEPS):
        phase = math.cos(2.0 * math.pi * (step + 0.5) / STEPS)
        post, stress = collide(state, label, drive, phase)
        total = total + stress
        padded = with_halo(post, (("gx", 1), ("gy", 2)), 1)
        moved = []
        for index in range(19):
            start_x = 1 - VELOCITY[index][0]
            start_y = 1 - VELOCITY[index][1]
            piece = padded[index, start_x : start_x + width, start_y : start_y + height, :]
            moved.append(jnp.roll(piece, VELOCITY[index][2], axis=2))
        state = jnp.stack(moved)
    momentum = momentum_of(state)
    block_x = width // 4
    block_y = height // 4
    slow_z = NZ // 4
    slow = (total / STEPS).reshape(6, block_x, 4, block_y, 4, slow_z, 4).mean(axis=(2, 4, 6))
    cosine_z, sine_z = tables(slow_z)
    spectrum = jnp.stack([product(slow, cosine_z), -product(slow, sine_z)])
    spectrum = lax.all_to_all(spectrum, "gy", split_axis=4, concat_axis=3, tiled=True)
    full_y = spectrum.shape[3]
    part_z = spectrum.shape[4]
    real, imag = transform(spectrum[0], spectrum[1], 2, False)
    spectrum = jnp.stack([real, imag]).reshape(2, 6, block_x, full_y * part_z)
    spectrum = lax.all_to_all(spectrum, "gx", split_axis=3, concat_axis=2, tiled=True)
    full_x = spectrum.shape[2]
    part_m = spectrum.shape[3]
    real, imag = transform(spectrum[0], spectrum[1], 1, False)
    wave_x = wavenumber(jnp.arange(full_x, dtype=jnp.int32), full_x).reshape(full_x, 1)
    flat = lax.axis_index("gx") * part_m + jnp.arange(part_m, dtype=jnp.int32)
    row_y = flat // part_z
    index_z = lax.axis_index("gy") * part_z + flat % part_z
    wave_y = wavenumber(row_y, full_y).reshape(1, part_m)
    wave_z = wavenumber(index_z, slow_z).reshape(1, part_m)
    waves = [wave_x, wave_y, wave_z]
    force_real = [
        waves[0] * imag[COMPONENT[first][0]]
        + waves[1] * imag[COMPONENT[first][1]]
        + waves[2] * imag[COMPONENT[first][2]]
        for first in range(3)
    ]
    force_imag = [
        -(
            waves[0] * real[COMPONENT[first][0]]
            + waves[1] * real[COMPONENT[first][1]]
            + waves[2] * real[COMPONENT[first][2]]
        )
        for first in range(3)
    ]
    wave_sq = wave_x * wave_x + wave_y * wave_y + wave_z * wave_z
    positive = wave_sq > 0
    safe = jnp.where(positive, wave_sq, 1.0)
    inner_real = waves[0] * force_real[0] + waves[1] * force_real[1] + waves[2] * force_real[2]
    inner_imag = waves[0] * force_imag[0] + waves[1] * force_imag[1] + waves[2] * force_imag[2]
    speed_real = jnp.stack(
        [
            jnp.where(
                positive,
                (force_real[first] - waves[first] * inner_real / safe) / (SLOW_VISCOSITY * safe),
                0.0,
            )
            for first in range(3)
        ]
    )
    speed_imag = jnp.stack(
        [
            jnp.where(
                positive,
                (force_imag[first] - waves[first] * inner_imag / safe) / (SLOW_VISCOSITY * safe),
                0.0,
            )
            for first in range(3)
        ]
    )
    real, imag = transform(speed_real, speed_imag, 1, True)
    result = lax.all_to_all(jnp.stack([real, imag]), "gx", split_axis=2, concat_axis=3, tiled=True)
    result = result.reshape(2, 3, block_x, full_y, part_z)
    real, imag = transform(result[0], result[1], 2, True)
    result = lax.all_to_all(jnp.stack([real, imag]), "gy", split_axis=3, concat_axis=4, tiled=True)
    running = (product(result[0], cosine_z) - product(result[1], sine_z)) / slow_z
    return (momentum, running)


def solution(mesh):
    in_specs = (P(None, "gx", "gy", None), P("gx", "gy", None), P(None, "gx", "gy", None))
    out_specs = (P(None, "gx", "gy", None), P(None, "gx", "gy", None))
    return jax.shard_map(local, mesh=mesh, in_specs=in_specs, out_specs=out_specs, check_vma=False)
```

profile of v0, /device:TPU:6, one launch (start us, length us, event | category | flops | bytes accessed | tf_op | source)
XLA Modules:
  0.0 232.1 jit_solution(13145048456317366882)
XLA Ops:
  0.6 0.8 constant_dynamic-update-slice_fusion.18
  1.4 0.7 constant_dynamic-update-slice_fusion.17
  2.1 0.7 constant_dynamic-update-slice_fusion.16
  2.9 0.7 constant_dynamic-update-slice_fusion.15
  3.6 0.7 constant_dynamic-update-slice_fusion.14
  4.3 0.7 constant_dynamic-update-slice_fusion.13
  5.0 0.7 constant_dynamic-update-slice_fusion.12
  5.7 0.7 constant_dynamic-update-slice_fusion.11
  6.5 0.7 constant_dynamic-update-slice_fusion.10
  8.0 0.8 copy-done.28
  11.3 10.2 %collective-permute-start = (f32[19,1,8,128]{3,2,1,0:T(8,128)S(1)}, f32[19,1,8,128]{3,2,1,0:T(8,128)S(1)}, u32[]{:S(2)}, u32[]{:S(2)}) collective-permute-start(f32[19,1,8,128]{3,2,1,0:T(8,128)S(1)} %get-tuple-element.234), channel_id=1, source_target_pairs={{8,0},{16,8},{24,16},{32,24},{40,32},{48,40},{56,48},{64,56},{72,6... | collective-permute-start | bytes 233480 | tf_op jit(solution)/shard_map/ppermute | solution.py:46
  21.5 1.9 collective-permute-start.1
  28.6 2.6 %collective-permute-done.1 = f32[19,1,8,128]{3,2,1,0:T(8,128)S(1)} collective-permute-done((f32[19,1,8,128]{3,2,1,0:T(8,128)S(1)}, f32[19,1,8,128]{3,2,1,0:T(8,128)S(1)}, u32[]{:S(2)}, u32[]{:S(2)}) %collective-permute-start.1) | collective-permute-done | bytes 77856 | tf_op jit(solution)/shard_map/ppermute | solution.py:44
  31.2 8.1 %collective-permute-start.3 = (f32[19,6,1,128]{3,2,1,0:T(1,128)S(1)}, f32[19,6,1,128]{3,2,1,0:T(1,128)S(1)}, u32[]{:S(2)}, u32[]{:S(2)}) collective-permute-start(f32[19,6,1,128]{3,2,1,0:T(1,128)S(1)} %get-tuple-element.202), channel_id=1, source_target_pairs={{0,1},{1,2},{2,3},{3,4},{4,5},{5,6},{6,7},{7,0},{8,9},{9,10},{10,1... | collective-permute-start | bytes 175112 | tf_op jit(solution)/shard_map/ppermute | solution.py:44
  39.4 1.9 collective-permute-start.2
  41.5 9.9 %collective-permute-done.2 = f32[19,6,1,128]{3,2,1,0:T(1,128)S(1)} collective-permute-done((f32[19,6,1,128]{3,2,1,0:T(1,128)S(1)}, f32[19,6,1,128]{3,2,1,0:T(1,128)S(1)}, u32[]{:S(2)}, u32[]{:S(2)}) %collective-permute-start.2) | collective-permute-done | bytes 58400 | tf_op jit(solution)/shard_map/ppermute | solution.py:46
  53.8 3.5 %collective-permute-start.4 = (f32[19,1,8,128]{3,2,1,0:T(8,128)S(1)}, f32[19,1,8,128]{3,2,1,0:T(8,128)S(1)}, u32[]{:S(2)}, u32[]{:S(2)}) collective-permute-start(f32[19,1,8,128]{3,2,1,0:T(8,128)S(1)} %get-tuple-element.230), channel_id=1, source_target_pairs={{8,0},{16,8},{24,16},{32,24},{40,32},{48,40},{56,48},{64,56},{72,6... | collective-permute-start | bytes 233480 | tf_op jit(solution)/shard_map/ppermute | solution.py:46
  57.3 1.9 collective-permute-start.5
  60.1 7.0 %collective-permute-done.5 = f32[19,1,8,128]{3,2,1,0:T(8,128)S(1)} collective-permute-done((f32[19,1,8,128]{3,2,1,0:T(8,128)S(1)}, f32[19,1,8,128]{3,2,1,0:T(8,128)S(1)}, u32[]{:S(2)}, u32[]{:S(2)}) %collective-permute-start.5) | collective-permute-done | bytes 77856 | tf_op jit(solution)/shard_map/ppermute | solution.py:44
  67.1 1.9 collective-permute-start.7
  69.1 3.9 %collective-permute-start.6 = (f32[19,6,1,128]{3,2,1,0:T(1,128)S(1)}, f32[19,6,1,128]{3,2,1,0:T(1,128)S(1)}, u32[]{:S(2)}, u32[]{:S(2)}) collective-permute-start(f32[19,6,1,128]{3,2,1,0:T(1,128)S(1)} %get-tuple-element.199), channel_id=1, source_target_pairs={{1,0},{2,1},{3,2},{4,3},{5,4},{6,5},{7,6},{0,7},{9,8},{10,9},{11,1... | collective-permute-start | bytes 175112 | tf_op jit(solution)/shard_map/ppermute | solution.py:46
  73.4 7.8 %collective-permute-done.6 = f32[19,6,1,128]{3,2,1,0:T(1,128)S(1)} collective-permute-done((f32[19,6,1,128]{3,2,1,0:T(1,128)S(1)}, f32[19,6,1,128]{3,2,1,0:T(1,128)S(1)}, u32[]{:S(2)}, u32[]{:S(2)}) %collective-permute-start.6) | collective-permute-done | bytes 58400 | tf_op jit(solution)/shard_map/ppermute | solution.py:46
  83.4 1.9 collective-permute-start.8
  85.4 2.4 %collective-permute-start.9 = (f32[19,1,8,128]{3,2,1,0:T(8,128)S(1)}, f32[19,1,8,128]{3,2,1,0:T(8,128)S(1)}, u32[]{:S(2)}, u32[]{:S(2)}) collective-permute-start(f32[19,1,8,128]{3,2,1,0:T(8,128)S(1)} %get-tuple-element.227), channel_id=1, source_target_pairs={{0,8},{8,16},{16,24},{24,32},{32,40},{40,48},{48,56},{56,64},{64,7... | collective-permute-start | bytes 233480 | tf_op jit(solution)/shard_map/ppermute | solution.py:44
  88.6 6.4 %collective-permute-done.9 = f32[19,1,8,128]{3,2,1,0:T(8,128)S(1)} collective-permute-done((f32[19,1,8,128]{3,2,1,0:T(8,128)S(1)}, f32[19,1,8,128]{3,2,1,0:T(8,128)S(1)}, u32[]{:S(2)}, u32[]{:S(2)}) %collective-permute-start.9) | collective-permute-done | bytes 77856 | tf_op jit(solution)/shard_map/ppermute | solution.py:44
  95.1 1.9 collective-permute-start.11
  97.0 4.1 %collective-permute-start.10 = (f32[19,6,1,128]{3,2,1,0:T(1,128)S(1)}, f32[19,6,1,128]{3,2,1,0:T(1,128)S(1)}, u32[]{:S(2)}, u32[]{:S(2)}) collective-permute-start(f32[19,6,1,128]{3,2,1,0:T(1,128)S(1)} %get-tuple-element.197), channel_id=1, source_target_pairs={{1,0},{2,1},{3,2},{4,3},{5,4},{6,5},{7,6},{0,7},{9,8},{10,9},{11,1... | collective-permute-start | bytes 175112 | tf_op jit(solution)/shard_map/ppermute | solution.py:46
  101.3 7.8 %collective-permute-done.10 = f32[19,6,1,128]{3,2,1,0:T(1,128)S(1)} collective-permute-done((f32[19,6,1,128]{3,2,1,0:T(1,128)S(1)}, f32[19,6,1,128]{3,2,1,0:T(1,128)S(1)}, u32[]{:S(2)}, u32[]{:S(2)}) %collective-permute-start.10) | collective-permute-done | bytes 58400 | tf_op jit(solution)/shard_map/ppermute | solution.py:46
  120.3 0.9 copy.159
  121.7 0.9 copy.160
  123.1 0.9 copy.150
  124.0 0.8 constant_dynamic-update-slice_fusion.163
  124.9 1.2 stack.378
  126.1 0.9 copy.151
  127.0 1.2 stack.379
  128.3 0.9 copy.152
  129.2 1.2 stack.380
  130.4 0.9 copy.153
  131.3 1.2 stack.381
  132.6 0.9 copy.154
  133.6 0.8 copy-done.1
  134.4 0.8 copy-done.2
  135.3 0.8 copy-done.3
  136.1 0.8 copy-done.4
  137.0 0.8 copy-done.5
  137.8 0.8 copy-done.6
  141.0 0.7 copy.171
  141.7 4.8 %all-to-all-start = ((f32[2,6,1,2,32]{1,3,2,0,4:T(2,128)}), f32[2,6,1,2,32]{1,3,2,0,4:T(2,128)S(1)}, u32[]{:S(2)}, u32[]{:S(2)}) async-start(f32[2,6,1,2,32]{1,3,2,0,4:T(2,128)} %copy.171), calls=%async_computation | async-start | bytes 131072 | tf_op jit(solution)/shard_map/all_to_all | solution.py:140
  146.6 8.2 %all-to-all-done = f32[2,6,1,2,32]{1,3,2,0,4:T(2,128)S(1)} async-done(((f32[2,6,1,2,32]{1,3,2,0,4:T(2,128)}), f32[2,6,1,2,32]{1,3,2,0,4:T(2,128)S(1)}, u32[]{:S(2)}, u32[]{:S(2)}) %all-to-all-start) | async-done | bytes 3104 | tf_op jit(solution)/shard_map/all_to_all | solution.py:140
  157.1 0.7 copy.179
  157.8 5.6 %all-to-all-start.1 = ((f32[2,6,1,64]{1,0,2,3:T(2,128)}), f32[2,6,1,64]{1,0,2,3:T(2,128)S(1)}, u32[]{:S(2)}, u32[]{:S(2)}) async-start(f32[2,6,1,64]{1,0,2,3:T(2,128)} %copy.179), calls=%async_computation.1 | async-start | bytes 131072 | tf_op jit(solution)/shard_map/all_to_all | solution.py:145
  164.5 8.8 %all-to-all-done.1 = f32[2,6,1,64]{1,0,2,3:T(2,128)S(1)} async-done(((f32[2,6,1,64]{1,0,2,3:T(2,128)}), f32[2,6,1,64]{1,0,2,3:T(2,128)S(1)}, u32[]{:S(2)}, u32[]{:S(2)}) %all-to-all-start.1) | async-done | bytes 3104 | tf_op jit(solution)/shard_map/all_to_all | solution.py:145
  175.7 0.7 copy.182
  176.5 4.6 %all-to-all-start.2 = ((f32[2,3,64,1]{1,3,0,2:T(1,128)}), f32[2,3,64,1]{1,3,0,2:T(1,128)S(1)}, u32[]{:S(2)}, u32[]{:S(2)}) async-start(f32[2,3,64,1]{1,3,0,2:T(1,128)} %copy.182), calls=%async_computation.2 | async-start | bytes 131072 | tf_op jit(solution)/shard_map/all_to_all | solution.py:196
  181.1 10.0 %all-to-all-done.2 = f32[2,3,64,1]{1,3,0,2:T(1,128)S(1)} async-done(((f32[2,3,64,1]{1,3,0,2:T(1,128)}), f32[2,3,64,1]{1,3,0,2:T(1,128)S(1)}, u32[]{:S(2)}, u32[]{:S(2)}) %all-to-all-start.2) | async-done | bytes 1568 | tf_op jit(solution)/shard_map/all_to_all | solution.py:196
  192.3 0.7 copy.187
  193.0 5.3 %all-to-all-start.3 = ((f32[2,3,1,16,4]{4,0,2,1,3:T(2,128)}), f32[2,3,1,16,4]{4,0,2,1,3:T(2,128)S(1)}, u32[]{:S(2)}, u32[]{:S(2)}) async-start(f32[2,3,1,16,4]{4,0,2,1,3:T(2,128)} %copy.187), calls=%async_computation.3 | async-start | bytes 98304 | tf_op jit(solution)/shard_map/all_to_all | solution.py:199
  198.3 2.3 %collective-permute-start.13 = (f32[19,1,8,128]{3,2,1,0:T(8,128)S(1)}, f32[19,1,8,128]{3,2,1,0:T(8,128)S(1)}, u32[]{:S(2)}, u32[]{:S(2)}) collective-permute-start(f32[19,1,8,128]{3,2,1,0:T(8,128)S(1)} %get-tuple-element.222), channel_id=1, source_target_pairs={{8,0},{16,8},{24,16},{32,24},{40,32},{48,40},{56,48},{64,56},{72,6... | collective-permute-start | bytes 233480 | tf_op jit(solution)/shard_map/ppermute | solution.py:46
  200.7 2.0 collective-permute-start.12
  202.7 3.8 %all-to-all-done.3 = f32[2,3,1,16,4]{4,0,2,1,3:T(2,128)S(1)} async-done(((f32[2,3,1,16,4]{4,0,2,1,3:T(2,128)}), f32[2,3,1,16,4]{4,0,2,1,3:T(2,128)S(1)}, u32[]{:S(2)}, u32[]{:S(2)}) %all-to-all-start.3) | async-done | bytes 1568 | tf_op jit(solution)/shard_map/all_to_all | solution.py:199
  207.8 2.5 %collective-permute-done.12 = f32[19,1,8,128]{3,2,1,0:T(8,128)S(1)} collective-permute-done((f32[19,1,8,128]{3,2,1,0:T(8,128)S(1)}, f32[19,1,8,128]{3,2,1,0:T(8,128)S(1)}, u32[]{:S(2)}, u32[]{:S(2)}) %collective-permute-start.12) | collective-permute-done | bytes 77856 | tf_op jit(solution)/shard_map/ppermute | solution.py:44
  210.4 7.3 %collective-permute-start.14 = (f32[19,6,1,128]{3,2,1,0:T(1,128)S(1)}, f32[19,6,1,128]{3,2,1,0:T(1,128)S(1)}, u32[]{:S(2)}, u32[]{:S(2)}) collective-permute-start(f32[19,6,1,128]{3,2,1,0:T(1,128)S(1)} %get-tuple-element.196), channel_id=1, source_target_pairs={{0,1},{1,2},{2,3},{3,4},{4,5},{5,6},{6,7},{7,0},{8,9},{9,10},{10,1... | collective-permute-start | bytes 175112 | tf_op jit(solution)/shard_map/ppermute | solution.py:44
  217.7 1.9 collective-permute-start.15
  219.6 10.1 %collective-permute-done.15 = f32[19,6,1,128]{3,2,1,0:T(1,128)S(1)} collective-permute-done((f32[19,6,1,128]{3,2,1,0:T(1,128)S(1)}, f32[19,6,1,128]{3,2,1,0:T(1,128)S(1)}, u32[]{:S(2)}, u32[]{:S(2)}) %collective-permute-start.15) | collective-permute-done | bytes 58400 | tf_op jit(solution)/shard_map/ppermute | solution.py:46
  (402 shorter events, 39.9 us)
Async XLA Ops:
  0.6 7.3 %copy-start = (f32[19,4,8,128]{3,2,1,0:T(8,128)S(1)}, f32[19,4,8,128]{3,2,1,0:T(8,128)}, u32[]{:S(2)}) copy-start(f32[19,4,8,128]{3,2,1,0:T(8,128)} %param.22) | copy-start | bytes 933892
  8.0 0.8 copy-start.28
  8.8 0.7 copy-start.29
  8.8 0.7 copy-start.30
  8.8 0.7 copy-start.32
  9.4 0.7 copy-start.34
  10.2 1.1 copy-start.19
  10.2 0.7 copy-start.35
  10.2 0.7 copy-start.37
  11.3 17.2 %collective-permute-start = (f32[19,1,8,128]{3,2,1,0:T(8,128)S(1)}, f32[19,1,8,128]{3,2,1,0:T(8,128)S(1)}, u32[]{:S(2)}, u32[]{:S(2)}) collective-permute-start(f32[19,1,8,128]{3,2,1,0:T(8,128)S(1)} %get-tuple-element.234), channel_id=1, source_target_pairs={{8,0},{16,8},{24,16},{32,24},{40,32},{48,40},{56,48},{64,56},{72,6... | collective-permute-start | bytes 233480 | tf_op jit(solution)/shard_map/ppermute | solution.py:46
  21.5 9.6 %collective-permute-start.1 = (f32[19,1,8,128]{3,2,1,0:T(8,128)S(1)}, f32[19,1,8,128]{3,2,1,0:T(8,128)S(1)}, u32[]{:S(2)}, u32[]{:S(2)}) collective-permute-start(f32[19,1,8,128]{3,2,1,0:T(8,128)S(1)} %get-tuple-element.235), channel_id=1, source_target_pairs={{0,8},{8,16},{16,24},{24,32},{32,40},{40,48},{48,56},{56,64},{64,7... | collective-permute-start | bytes 233480 | tf_op jit(solution)/shard_map/ppermute | solution.py:44
  31.2 10.1 %collective-permute-start.3 = (f32[19,6,1,128]{3,2,1,0:T(1,128)S(1)}, f32[19,6,1,128]{3,2,1,0:T(1,128)S(1)}, u32[]{:S(2)}, u32[]{:S(2)}) collective-permute-start(f32[19,6,1,128]{3,2,1,0:T(1,128)S(1)} %get-tuple-element.202), channel_id=1, source_target_pairs={{0,1},{1,2},{2,3},{3,4},{4,5},{5,6},{6,7},{7,0},{8,9},{9,10},{10,1... | collective-permute-start | bytes 175112 | tf_op jit(solution)/shard_map/ppermute | solution.py:44
  39.4 12.1 %collective-permute-start.2 = (f32[19,6,1,128]{3,2,1,0:T(1,128)S(1)}, f32[19,6,1,128]{3,2,1,0:T(1,128)S(1)}, u32[]{:S(2)}, u32[]{:S(2)}) collective-permute-start(f32[19,6,1,128]{3,2,1,0:T(1,128)S(1)} %get-tuple-element.201), channel_id=1, source_target_pairs={{1,0},{2,1},{3,2},{4,3},{5,4},{6,5},{7,6},{0,7},{9,8},{10,9},{11,1... | collective-permute-start | bytes 175112 | tf_op jit(solution)/shard_map/ppermute | solution.py:46
  53.8 6.3 %collective-permute-start.4 = (f32[19,1,8,128]{3,2,1,0:T(8,128)S(1)}, f32[19,1,8,128]{3,2,1,0:T(8,128)S(1)}, u32[]{:S(2)}, u32[]{:S(2)}) collective-permute-start(f32[19,1,8,128]{3,2,1,0:T(8,128)S(1)} %get-tuple-element.230), channel_id=1, source_target_pairs={{8,0},{16,8},{24,16},{32,24},{40,32},{48,40},{56,48},{64,56},{72,6... | collective-permute-start | bytes 233480 | tf_op jit(solution)/shard_map/ppermute | solution.py:46
  57.3 9.8 %collective-permute-start.5 = (f32[19,1,8,128]{3,2,1,0:T(8,128)S(1)}, f32[19,1,8,128]{3,2,1,0:T(8,128)S(1)}, u32[]{:S(2)}, u32[]{:S(2)}) collective-permute-start(f32[19,1,8,128]{3,2,1,0:T(8,128)S(1)} %get-tuple-element.231), channel_id=1, source_target_pairs={{0,8},{8,16},{16,24},{24,32},{32,40},{40,48},{48,56},{56,64},{64,7... | collective-permute-start | bytes 233480 | tf_op jit(solution)/shard_map/ppermute | solution.py:44
  67.1 6.1 %collective-permute-start.7 = (f32[19,6,1,128]{3,2,1,0:T(1,128)S(1)}, f32[19,6,1,128]{3,2,1,0:T(1,128)S(1)}, u32[]{:S(2)}, u32[]{:S(2)}) collective-permute-start(f32[19,6,1,128]{3,2,1,0:T(1,128)S(1)} %get-tuple-element.200), channel_id=1, source_target_pairs={{0,1},{1,2},{2,3},{3,4},{4,5},{5,6},{6,7},{7,0},{8,9},{9,10},{10,1... | collective-permute-start | bytes 175112 | tf_op jit(solution)/shard_map/ppermute | solution.py:44
  69.1 12.1 %collective-permute-start.6 = (f32[19,6,1,128]{3,2,1,0:T(1,128)S(1)}, f32[19,6,1,128]{3,2,1,0:T(1,128)S(1)}, u32[]{:S(2)}, u32[]{:S(2)}) collective-permute-start(f32[19,6,1,128]{3,2,1,0:T(1,128)S(1)} %get-tuple-element.199), channel_id=1, source_target_pairs={{1,0},{2,1},{3,2},{4,3},{5,4},{6,5},{7,6},{0,7},{9,8},{10,9},{11,1... | collective-permute-start | bytes 175112 | tf_op jit(solution)/shard_map/ppermute | solution.py:46
  83.4 5.2 %collective-permute-start.8 = (f32[19,1,8,128]{3,2,1,0:T(8,128)S(1)}, f32[19,1,8,128]{3,2,1,0:T(8,128)S(1)}, u32[]{:S(2)}, u32[]{:S(2)}) collective-permute-start(f32[19,1,8,128]{3,2,1,0:T(8,128)S(1)} %get-tuple-element.226), channel_id=1, source_target_pairs={{8,0},{16,8},{24,16},{32,24},{40,32},{48,40},{56,48},{64,56},{72,6... | collective-permute-start | bytes 233480 | tf_op jit(solution)/shard_map/ppermute | solution.py:46
  85.4 9.6 %collective-permute-start.9 = (f32[19,1,8,128]{3,2,1,0:T(8,128)S(1)}, f32[19,1,8,128]{3,2,1,0:T(8,128)S(1)}, u32[]{:S(2)}, u32[]{:S(2)}) collective-permute-start(f32[19,1,8,128]{3,2,1,0:T(8,128)S(1)} %get-tuple-element.227), channel_id=1, source_target_pairs={{0,8},{8,16},{16,24},{24,32},{32,40},{40,48},{48,56},{56,64},{64,7... | collective-permute-start | bytes 233480 | tf_op jit(solution)/shard_map/ppermute | solution.py:44
  95.1 6.1 %collective-permute-start.11 = (f32[19,6,1,128]{3,2,1,0:T(1,128)S(1)}, f32[19,6,1,128]{3,2,1,0:T(1,128)S(1)}, u32[]{:S(2)}, u32[]{:S(2)}) collective-permute-start(f32[19,6,1,128]{3,2,1,0:T(1,128)S(1)} %get-tuple-element.198), channel_id=1, source_target_pairs={{0,1},{1,2},{2,3},{3,4},{4,5},{5,6},{6,7},{7,0},{8,9},{9,10},{10,1... | collective-permute-start | bytes 175112 | tf_op jit(solution)/shard_map/ppermute | solution.py:44
  97.0 12.1 %collective-permute-start.10 = (f32[19,6,1,128]{3,2,1,0:T(1,128)S(1)}, f32[19,6,1,128]{3,2,1,0:T(1,128)S(1)}, u32[]{:S(2)}, u32[]{:S(2)}) collective-permute-start(f32[19,6,1,128]{3,2,1,0:T(1,128)S(1)} %get-tuple-element.197), channel_id=1, source_target_pairs={{1,0},{2,1},{3,2},{4,3},{5,4},{6,5},{7,6},{0,7},{9,8},{10,9},{11,1... | collective-permute-start | bytes 175112 | tf_op jit(solution)/shard_map/ppermute | solution.py:46
  101.2 9.5 %copy-start.21 = (f32[1,4,8,128]{3,2,1,0:T(8,128)}, f32[1,4,8,128]{3,2,1,0:T(8,128)S(1)}, u32[]{:S(2)}) copy-start(f32[1,4,8,128]{3,2,1,0:T(8,128)S(1)} %get-tuple-element.78) | copy-start | bytes 49156
  109.1 1.6 copy-start.23
  109.2 1.5 copy-start.25
  110.1 0.7 copy-start.9
  110.2 0.6 copy-start.7
  110.3 0.6 copy-start.13
  110.3 0.6 copy-start.11
  110.4 0.6 copy-start.15
  110.6 0.6 copy-start.17
  133.6 0.8 copy-start.1
  134.4 0.8 copy-start.2
  135.3 0.8 copy-start.3
  136.1 0.8 copy-start.4
  136.9 0.8 copy-start.5
  137.8 0.8 copy-start.6
  139.3 0.7 copy-start.24
  139.3 0.7 copy-start.22
  139.3 0.8 copy-start.26
  139.3 0.8 copy-start.27
  140.0 0.7 copy-start.12
  140.0 0.7 copy-start.14
  140.0 0.7 copy-start.16
  140.0 0.8 copy-start.18
  140.1 0.7 copy-start.8
  140.1 0.7 copy-start.10
  141.7 13.0 %all-to-all-start = ((f32[2,6,1,2,32]{1,3,2,0,4:T(2,128)}), f32[2,6,1,2,32]{1,3,2,0,4:T(2,128)S(1)}, u32[]{:S(2)}, u32[]{:S(2)}) async-start(f32[2,6,1,2,32]{1,3,2,0,4:T(2,128)} %copy.171), calls=%async_computation | async-start | bytes 131072 | tf_op jit(solution)/shard_map/all_to_all | solution.py:140
  155.6 7.8 %copy-start.38 = (f32[19]{0:T(128)S(1)}, f32[19]{0:T(128)}, u32[]{:S(2)}) copy-start(f32[19]{0:T(128)} %constant.177.clone) | copy-start | bytes 232
  157.8 5.7 %copy-start.20 = (f32[4,8,128]{2,1,0:T(8,128)S(1)}, f32[4,8,128]{2,1,0:T(8,128)}, u32[]{:S(2)}) copy-start(f32[4,8,128]{2,1,0:T(8,128)} %copy-done.19) | copy-start | bytes 49156
  157.8 15.5 %all-to-all-start.1 = ((f32[2,6,1,64]{1,0,2,3:T(2,128)}), f32[2,6,1,64]{1,0,2,3:T(2,128)S(1)}, u32[]{:S(2)}, u32[]{:S(2)}) async-start(f32[2,6,1,64]{1,0,2,3:T(2,128)} %copy.179), calls=%async_computation.1 | async-start | bytes 131072 | tf_op jit(solution)/shard_map/all_to_all | solution.py:145
  163.4 0.7 copy-start.31
  163.5 0.7 copy-start.33
  163.5 0.7 copy-start.36
  176.5 14.6 %all-to-all-start.2 = ((f32[2,3,64,1]{1,3,0,2:T(1,128)}), f32[2,3,64,1]{1,3,0,2:T(1,128)S(1)}, u32[]{:S(2)}, u32[]{:S(2)}) async-start(f32[2,3,64,1]{1,3,0,2:T(1,128)} %copy.182), calls=%async_computation.2 | async-start | bytes 131072 | tf_op jit(solution)/shard_map/all_to_all | solution.py:196
  193.0 13.5 %all-to-all-start.3 = ((f32[2,3,1,16,4]{4,0,2,1,3:T(2,128)}), f32[2,3,1,16,4]{4,0,2,1,3:T(2,128)S(1)}, u32[]{:S(2)}, u32[]{:S(2)}) async-start(f32[2,3,1,16,4]{4,0,2,1,3:T(2,128)} %copy.187), calls=%async_computation.3 | async-start | bytes 98304 | tf_op jit(solution)/shard_map/all_to_all | solution.py:199
  198.3 9.4 %collective-permute-start.13 = (f32[19,1,8,128]{3,2,1,0:T(8,128)S(1)}, f32[19,1,8,128]{3,2,1,0:T(8,128)S(1)}, u32[]{:S(2)}, u32[]{:S(2)}) collective-permute-start(f32[19,1,8,128]{3,2,1,0:T(8,128)S(1)} %get-tuple-element.222), channel_id=1, source_target_pairs={{8,0},{16,8},{24,16},{32,24},{40,32},{48,40},{56,48},{64,56},{72,6... | collective-permute-start | bytes 233480 | tf_op jit(solution)/shard_map/ppermute | solution.py:46
  200.7 9.6 %collective-permute-start.12 = (f32[19,1,8,128]{3,2,1,0:T(8,128)S(1)}, f32[19,1,8,128]{3,2,1,0:T(8,128)S(1)}, u32[]{:S(2)}, u32[]{:S(2)}) collective-permute-start(f32[19,1,8,128]{3,2,1,0:T(8,128)S(1)} %get-tuple-element.223), channel_id=1, source_target_pairs={{0,8},{8,16},{16,24},{24,32},{32,40},{40,48},{48,56},{56,64},{64,7... | collective-permute-start | bytes 233480 | tf_op jit(solution)/shard_map/ppermute | solution.py:44
  210.4 9.2 %collective-permute-start.14 = (f32[19,6,1,128]{3,2,1,0:T(1,128)S(1)}, f32[19,6,1,128]{3,2,1,0:T(1,128)S(1)}, u32[]{:S(2)}, u32[]{:S(2)}) collective-permute-start(f32[19,6,1,128]{3,2,1,0:T(1,128)S(1)} %get-tuple-element.196), channel_id=1, source_target_pairs={{0,1},{1,2},{2,3},{3,4},{4,5},{5,6},{6,7},{7,0},{8,9},{9,10},{10,1... | collective-permute-start | bytes 175112 | tf_op jit(solution)/shard_map/ppermute | solution.py:44
  217.7 12.1 %collective-permute-start.15 = (f32[19,6,1,128]{3,2,1,0:T(1,128)S(1)}, f32[19,6,1,128]{3,2,1,0:T(1,128)S(1)}, u32[]{:S(2)}, u32[]{:S(2)}) collective-permute-start(f32[19,6,1,128]{3,2,1,0:T(1,128)S(1)} %get-tuple-element.195), channel_id=1, source_target_pairs={{1,0},{2,1},{3,2},{4,3},{5,4},{6,5},{7,6},{0,7},{9,8},{10,9},{11,1... | collective-permute-start | bytes 175112 | tf_op jit(solution)/shard_map/ppermute | solution.py:46
where the time goes:
time: 234 us; the launch traced here: 232 us
  waiting for transfers between devices  85.1 us (36%)
  starting transfers between devices  77.7 us (33%)
  local copies, waits for them, and re-layouts  53.3 us (23%)
  other arithmetic  8.57 us (4%)
  matrix products  4.96 us (2%)
  between operations  2.44 us (1%)
    ppermute x8, waiting for transfers between devices, with_halo(): lax.ppermute(head, axis, [((i + 1) % count, i) for i in range(count)])  35.6 us
    ppermute x8, starting transfers between devices, with_halo(): lax.ppermute(head, axis, [((i + 1) % count, i) for i in range(count)])  29.9 us
    ppermute x8, starting transfers between devices, with_halo(): lax.ppermute(tail, axis, [(i, (i + 1) % count) for i in range(count)])  27.5 us
    another operation x52, local copies, waits for them, and re-layouts, collide(): jnp.stack([moment[first] * moment[later] / density * fluid for first, lat...  26.4 us
    unnamed x172, local copies, waits for them, and re-layouts  19.1 us
    ppermute x8, waiting for transfers between devices, with_halo(): lax.ppermute(tail, axis, [(i, (i + 1) % count) for i in range(count)])  18.7 us
    all_to_all x1, waiting for transfers between devices, local(): lax.all_to_all(jnp.stack([real, imag]), 'gx', split_axis=2, concat_axis=3...  9.99 us
    all_to_all x1, waiting for transfers between devices, local(): lax.all_to_all(spectrum, 'gx', split_axis=3, concat_axis=2, tiled=True)  8.78 us
  transfers between devices with their start and end apart: 20, of which 13 were waited for; matrix products, arithmetic and copies ran while one was open for 4% of the time, Pallas kernels for 0%

commit v1 on v0

--- a/solution.py
+++ b/solution.py
@@ -193,7 +193,12 @@
         ]
     )
     real, imag = transform(speed_real, speed_imag, 1, True)
-    result = lax.all_to_all(jnp.stack([real, imag]), "gx", split_axis=2, concat_axis=3, tiled=True)
+    result = jnp.concatenate(
+        lax.all_to_all(
+            jnp.stack(jnp.split(jnp.stack([real, imag]), lax.axis_size("gx"), axis=2)), "gx", 0, 0
+        ),
+        axis=3,
+    )
     result = result.reshape(2, 3, block_x, full_y, part_z)
     real, imag = transform(result[0], result[1], 2, True)
     result = lax.all_to_all(jnp.stack([real, imag]), "gy", split_axis=3, concat_axis=4, tiled=True)

time: 234 us -> 272 us (1.16)
  local copies, waits for them, and re-layouts: 53.3 us -> 89.1 us
    unnamed x172 -> x235, local copies, waits for them, and re-layouts: 19.1 us -> 55.1 us
  transfers between devices with their start and end apart: 20 -> 20, of which waited for: 13 -> 13; matrix products, arithmetic and copies ran while one was open for 4% -> 3% of each run, Pallas kernels for 0% -> 0%
where the time goes in v1:
time: 272 us; the launch traced here: 269 us
  local copies, waits for them, and re-layouts  89.1 us (33%)
  waiting for transfers between devices  85.1 us (31%)
  starting transfers between devices  77.8 us (29%)
  other arithmetic  10 us (4%)
  matrix products  4.96 us (2%)
    unnamed x235, local copies, waits for them, and re-layouts  55.1 us
    ppermute x8, waiting for transfers between devices, with_halo(): lax.ppermute(head, axis, [((i + 1) % count, i) for i in range(count)])  35.6 us
    ppermute x8, starting transfers between devices, with_halo(): lax.ppermute(head, axis, [((i + 1) % count, i) for i in range(count)])  29.9 us
    ppermute x8, starting transfers between devices, with_halo(): lax.ppermute(tail, axis, [(i, (i + 1) % count) for i in range(count)])  27.5 us
    another operation x52, local copies, waits for them, and re-layouts, collide(): jnp.stack([moment[first] * moment[later] / density * fluid for first, lat...  26.4 us
    ppermute x8, waiting for transfers between devices, with_halo(): lax.ppermute(tail, axis, [(i, (i + 1) % count) for i in range(count)])  18.7 us
    all_to_all x1, waiting for transfers between devices, local(): lax.all_to_all(jnp.stack(jnp.split(jnp.stack([real, imag]), lax.axis_size...  10 us
    all_to_all x1, waiting for transfers between devices, local(): lax.all_to_all(spectrum, 'gx', split_axis=3, concat_axis=2, tiled=True)  8.79 us
  transfers between devices with their start and end apart: 20, of which 13 were waited for; matrix products, arithmetic and copies ran while one was open for 3% of the time, Pallas kernels for 0%

profile of v1, /device:TPU:6, one launch (start us, length us, event | category | flops | bytes accessed | tf_op | source)
XLA Modules:
  0.0 269.4 jit_solution(12025061787345648124)
XLA Ops:
  0.6 0.8 constant_dynamic-update-slice_fusion.18
  1.4 0.7 constant_dynamic-update-slice_fusion.17
  2.1 0.7 constant_dynamic-update-slice_fusion.16
  2.9 0.7 constant_dynamic-update-slice_fusion.15
  3.6 0.7 constant_dynamic-update-slice_fusion.14
  4.3 0.7 constant_dynamic-update-slice_fusion.13
  5.0 0.7 constant_dynamic-update-slice_fusion.12
  5.7 0.7 constant_dynamic-update-slice_fusion.11
  6.5 0.7 constant_dynamic-update-slice_fusion.10
  7.2 0.7 constant_dynamic-update-slice_fusion.9
  8.0 0.8 copy-done.28
  11.3 10.2 %collective-permute-start = (f32[19,1,8,128]{3,2,1,0:T(8,128)S(1)}, f32[19,1,8,128]{3,2,1,0:T(8,128)S(1)}, u32[]{:S(2)}, u32[]{:S(2)}) collective-permute-start(f32[19,1,8,128]{3,2,1,0:T(8,128)S(1)} %get-tuple-element.301), channel_id=1, source_target_pairs={{8,0},{16,8},{24,16},{32,24},{40,32},{48,40},{56,48},{64,56},{72,6... | collective-permute-start | bytes 233480 | tf_op jit(solution)/shard_map/ppermute | solution.py:46
  21.5 1.9 collective-permute-start.1
  28.6 2.6 collective-permute-done.1
  31.2 8.1 %collective-permute-start.3 = (f32[19,6,1,128]{3,2,1,0:T(1,128)S(1)}, f32[19,6,1,128]{3,2,1,0:T(1,128)S(1)}, u32[]{:S(2)}, u32[]{:S(2)}) collective-permute-start(f32[19,6,1,128]{3,2,1,0:T(1,128)S(1)} %get-tuple-element.269), channel_id=1, source_target_pairs={{0,1},{1,2},{2,3},{3,4},{4,5},{5,6},{6,7},{7,0},{8,9},{9,10},{10,1... | collective-permute-start | bytes 175112 | tf_op jit(solution)/shard_map/ppermute | solution.py:44
  39.4 1.9 collective-permute-start.2
  41.5 9.9 %collective-permute-done.2 = f32[19,6,1,128]{3,2,1,0:T(1,128)S(1)} collective-permute-done((f32[19,6,1,128]{3,2,1,0:T(1,128)S(1)}, f32[19,6,1,128]{3,2,1,0:T(1,128)S(1)}, u32[]{:S(2)}, u32[]{:S(2)}) %collective-permute-start.2) | collective-permute-done | bytes 58400 | tf_op jit(solution)/shard_map/ppermute | solution.py:46
  53.8 3.5 %collective-permute-start.4 = (f32[19,1,8,128]{3,2,1,0:T(8,128)S(1)}, f32[19,1,8,128]{3,2,1,0:T(8,128)S(1)}, u32[]{:S(2)}, u32[]{:S(2)}) collective-permute-start(f32[19,1,8,128]{3,2,1,0:T(8,128)S(1)} %get-tuple-element.297), channel_id=1, source_target_pairs={{8,0},{16,8},{24,16},{32,24},{40,32},{48,40},{56,48},{64,56},{72,6... | collective-permute-start | bytes 233480 | tf_op jit(solution)/shard_map/ppermute | solution.py:46
  57.3 1.9 collective-permute-start.5
  60.1 7.0 %collective-permute-done.5 = f32[19,1,8,128]{3,2,1,0:T(8,128)S(1)} collective-permute-done((f32[19,1,8,128]{3,2,1,0:T(8,128)S(1)}, f32[19,1,8,128]{3,2,1,0:T(8,128)S(1)}, u32[]{:S(2)}, u32[]{:S(2)}) %collective-permute-start.5) | collective-permute-done | bytes 77856 | tf_op jit(solution)/shard_map/ppermute | solution.py:44
  67.1 1.9 collective-permute-start.7
  69.1 3.9 %collective-permute-start.6 = (f32[19,6,1,128]{3,2,1,0:T(1,128)S(1)}, f32[19,6,1,128]{3,2,1,0:T(1,128)S(1)}, u32[]{:S(2)}, u32[]{:S(2)}) collective-permute-start(f32[19,6,1,128]{3,2,1,0:T(1,128)S(1)} %get-tuple-element.266), channel_id=1, source_target_pairs={{1,0},{2,1},{3,2},{4,3},{5,4},{6,5},{7,6},{0,7},{9,8},{10,9},{11,1... | collective-permute-start | bytes 175112 | tf_op jit(solution)/shard_map/ppermute | solution.py:46
  73.4 7.8 %collective-permute-done.6 = f32[19,6,1,128]{3,2,1,0:T(1,128)S(1)} collective-permute-done((f32[19,6,1,128]{3,2,1,0:T(1,128)S(1)}, f32[19,6,1,128]{3,2,1,0:T(1,128)S(1)}, u32[]{:S(2)}, u32[]{:S(2)}) %collective-permute-start.6) | collective-permute-done | bytes 58400 | tf_op jit(solution)/shard_map/ppermute | solution.py:46
  83.4 1.9 collective-permute-start.8
  85.4 2.4 collective-permute-start.9
  88.6 6.4 %collective-permute-done.9 = f32[19,1,8,128]{3,2,1,0:T(8,128)S(1)} collective-permute-done((f32[19,1,8,128]{3,2,1,0:T(8,128)S(1)}, f32[19,1,8,128]{3,2,1,0:T(8,128)S(1)}, u32[]{:S(2)}, u32[]{:S(2)}) %collective-permute-start.9) | collective-permute-done | bytes 77856 | tf_op jit(solution)/shard_map/ppermute | solution.py:44
  95.1 1.9 collective-permute-start.11
  97.0 4.1 %collective-permute-start.10 = (f32[19,6,1,128]{3,2,1,0:T(1,128)S(1)}, f32[19,6,1,128]{3,2,1,0:T(1,128)S(1)}, u32[]{:S(2)}, u32[]{:S(2)}) collective-permute-start(f32[19,6,1,128]{3,2,1,0:T(1,128)S(1)} %get-tuple-element.264), channel_id=1, source_target_pairs={{1,0},{2,1},{3,2},{4,3},{5,4},{6,5},{7,6},{0,7},{9,8},{10,9},{11,1... | collective-permute-start | bytes 175112 | tf_op jit(solution)/shard_map/ppermute | solution.py:46
  101.3 7.8 %collective-permute-done.10 = f32[19,6,1,128]{3,2,1,0:T(1,128)S(1)} collective-permute-done((f32[19,6,1,128]{3,2,1,0:T(1,128)S(1)}, f32[19,6,1,128]{3,2,1,0:T(1,128)S(1)}, u32[]{:S(2)}, u32[]{:S(2)}) %collective-permute-start.10) | collective-permute-done | bytes 58400 | tf_op jit(solution)/shard_map/ppermute | solution.py:46
  120.3 0.9 copy.509
  121.7 0.9 copy.510
  123.1 0.9 copy.500
  124.0 0.8 constant_dynamic-update-slice_fusion.163
  124.9 1.2 stack.573
  126.1 0.9 copy.501
  127.0 1.2 stack.574
  128.2 0.9 copy.502
  129.1 1.2 stack.575
  130.4 0.9 copy.503
  131.3 1.2 stack.576
  132.5 0.9 copy.504
  133.5 0.8 copy-done.1
  134.4 0.8 copy-done.2
  135.2 0.8 copy-done.3
  136.1 0.8 copy-done.4
  136.9 0.8 copy-done.5
  137.7 0.8 copy-done.6
  140.9 0.7 copy.521
  141.7 4.8 %all-to-all-start = ((f32[2,6,1,2,32]{1,3,2,0,4:T(2,128)}), f32[2,6,1,2,32]{1,3,2,0,4:T(2,128)S(1)}, u32[]{:S(2)}, u32[]{:S(2)}) async-start(f32[2,6,1,2,32]{1,3,2,0,4:T(2,128)} %copy.521), calls=%async_computation | async-start | bytes 131072 | tf_op jit(solution)/shard_map/all_to_all | solution.py:140
  146.5 8.2 %all-to-all-done = f32[2,6,1,2,32]{1,3,2,0,4:T(2,128)S(1)} async-done(((f32[2,6,1,2,32]{1,3,2,0,4:T(2,128)}), f32[2,6,1,2,32]{1,3,2,0,4:T(2,128)S(1)}, u32[]{:S(2)}, u32[]{:S(2)}) %all-to-all-start) | async-done | bytes 3104 | tf_op jit(solution)/shard_map/all_to_all | solution.py:140
  157.0 0.7 copy.529
  157.8 5.6 %all-to-all-start.1 = ((f32[2,6,1,64]{1,0,2,3:T(2,128)}), f32[2,6,1,64]{1,0,2,3:T(2,128)S(1)}, u32[]{:S(2)}, u32[]{:S(2)}) async-start(f32[2,6,1,64]{1,0,2,3:T(2,128)} %copy.529), calls=%async_computation.1 | async-start | bytes 131072 | tf_op jit(solution)/shard_map/all_to_all | solution.py:145
  164.5 8.8 %all-to-all-done.1 = f32[2,6,1,64]{1,0,2,3:T(2,128)S(1)} async-done(((f32[2,6,1,64]{1,0,2,3:T(2,128)}), f32[2,6,1,64]{1,0,2,3:T(2,128)S(1)}, u32[]{:S(2)}, u32[]{:S(2)}) %all-to-all-start.1) | async-done | bytes 3104 | tf_op jit(solution)/shard_map/all_to_all | solution.py:145
  213.8 4.6 %all-to-all-start.2 = ((f32[64,2,3,1,1]{2,1,4,3,0:T(2,128)}), f32[64,2,3,1,1]{2,1,4,3,0:T(2,128)S(1)}, u32[]{:S(2)}, u32[]{:S(2)}) async-start(f32[64,2,3,1,1]{2,1,4,3,0:T(2,128)} %constant_dynamic-update-slice_fusion.176), calls=%async_computation.2 | async-start | bytes 131072 | tf_op jit(solution)/shard_map/all_to_all | solution.py:197
  218.4 10.0 %all-to-all-done.2 = f32[64,2,3,1,1]{2,1,4,3,0:T(2,128)S(1)} async-done(((f32[64,2,3,1,1]{2,1,4,3,0:T(2,128)}), f32[64,2,3,1,1]{2,1,4,3,0:T(2,128)S(1)}, u32[]{:S(2)}, u32[]{:S(2)}) %all-to-all-start.2) | async-done | bytes 1568 | tf_op jit(solution)/shard_map/all_to_all | solution.py:197
  229.6 0.7 copy.536
  230.3 5.3 %all-to-all-start.3 = ((f32[2,3,1,16,4]{4,0,2,1,3:T(2,128)}), f32[2,3,1,16,4]{4,0,2,1,3:T(2,128)S(1)}, u32[]{:S(2)}, u32[]{:S(2)}) async-start(f32[2,3,1,16,4]{4,0,2,1,3:T(2,128)} %copy.536), calls=%async_computation.3 | async-start | bytes 98304 | tf_op jit(solution)/shard_map/all_to_all | solution.py:204
  235.7 2.3 collective-permute-start.13
  238.0 2.0 collective-permute-start.12
  240.0 3.8 %all-to-all-done.3 = f32[2,3,1,16,4]{4,0,2,1,3:T(2,128)S(1)} async-done(((f32[2,3,1,16,4]{4,0,2,1,3:T(2,128)}), f32[2,3,1,16,4]{4,0,2,1,3:T(2,128)S(1)}, u32[]{:S(2)}, u32[]{:S(2)}) %all-to-all-start.3) | async-done | bytes 1568 | tf_op jit(solution)/shard_map/all_to_all | solution.py:204
  245.1 2.5 collective-permute-done.12
  247.7 7.3 %collective-permute-start.14 = (f32[19,6,1,128]{3,2,1,0:T(1,128)S(1)}, f32[19,6,1,128]{3,2,1,0:T(1,128)S(1)}, u32[]{:S(2)}, u32[]{:S(2)}) collective-permute-start(f32[19,6,1,128]{3,2,1,0:T(1,128)S(1)} %get-tuple-element.263), channel_id=1, source_target_pairs={{0,1},{1,2},{2,3},{3,4},{4,5},{5,6},{6,7},{7,0},{8,9},{9,10},{10,1... | collective-permute-start | bytes 175112 | tf_op jit(solution)/shard_map/ppermute | solution.py:44
  255.0 1.9 collective-permute-start.15
  257.0 10.1 %collective-permute-done.15 = f32[19,6,1,128]{3,2,1,0:T(1,128)S(1)} collective-permute-done((f32[19,6,1,128]{3,2,1,0:T(1,128)S(1)}, f32[19,6,1,128]{3,2,1,0:T(1,128)S(1)}, u32[]{:S(2)}, u32[]{:S(2)}) %collective-permute-start.15) | collective-permute-done | bytes 58400 | tf_op jit(solution)/shard_map/ppermute | solution.py:46
  (472 shorter events, 77.2 us)
Async XLA Ops:
  0.6 7.3 %copy-start = (f32[19,4,8,128]{3,2,1,0:T(8,128)S(1)}, f32[19,4,8,128]{3,2,1,0:T(8,128)}, u32[]{:S(2)}) copy-start(f32[19,4,8,128]{3,2,1,0:T(8,128)} %param.22) | copy-start | bytes 933892
  8.0 0.8 copy-start.28
  8.8 0.7 copy-start.29
  8.8 0.7 copy-start.30
  8.8 0.7 copy-start.32
  9.4 0.7 copy-start.34
  10.2 1.1 copy-start.19
  10.2 0.7 copy-start.35
  10.2 0.7 copy-start.37
  11.3 17.2 %collective-permute-start = (f32[19,1,8,128]{3,2,1,0:T(8,128)S(1)}, f32[19,1,8,128]{3,2,1,0:T(8,128)S(1)}, u32[]{:S(2)}, u32[]{:S(2)}) collective-permute-start(f32[19,1,8,128]{3,2,1,0:T(8,128)S(1)} %get-tuple-element.301), channel_id=1, source_target_pairs={{8,0},{16,8},{24,16},{32,24},{40,32},{48,40},{56,48},{64,56},{72,6... | collective-permute-start | bytes 233480 | tf_op jit(solution)/shard_map/ppermute | solution.py:46
  21.5 9.6 %collective-permute-start.1 = (f32[19,1,8,128]{3,2,1,0:T(8,128)S(1)}, f32[19,1,8,128]{3,2,1,0:T(8,128)S(1)}, u32[]{:S(2)}, u32[]{:S(2)}) collective-permute-start(f32[19,1,8,128]{3,2,1,0:T(8,128)S(1)} %get-tuple-element.302), channel_id=1, source_target_pairs={{0,8},{8,16},{16,24},{24,32},{32,40},{40,48},{48,56},{56,64},{64,7... | collective-permute-start | bytes 233480 | tf_op jit(solution)/shard_map/ppermute | solution.py:44
  31.2 10.1 %collective-permute-start.3 = (f32[19,6,1,128]{3,2,1,0:T(1,128)S(1)}, f32[19,6,1,128]{3,2,1,0:T(1,128)S(1)}, u32[]{:S(2)}, u32[]{:S(2)}) collective-permute-start(f32[19,6,1,128]{3,2,1,0:T(1,128)S(1)} %get-tuple-element.269), channel_id=1, source_target_pairs={{0,1},{1,2},{2,3},{3,4},{4,5},{5,6},{6,7},{7,0},{8,9},{9,10},{10,1... | collective-permute-start | bytes 175112 | tf_op jit(solution)/shard_map/ppermute | solution.py:44
  39.4 12.1 %collective-permute-start.2 = (f32[19,6,1,128]{3,2,1,0:T(1,128)S(1)}, f32[19,6,1,128]{3,2,1,0:T(1,128)S(1)}, u32[]{:S(2)}, u32[]{:S(2)}) collective-permute-start(f32[19,6,1,128]{3,2,1,0:T(1,128)S(1)} %get-tuple-element.268), channel_id=1, source_target_pairs={{1,0},{2,1},{3,2},{4,3},{5,4},{6,5},{7,6},{0,7},{9,8},{10,9},{11,1... | collective-permute-start | bytes 175112 | tf_op jit(solution)/shard_map/ppermute | solution.py:46
  53.8 6.3 %collective-permute-start.4 = (f32[19,1,8,128]{3,2,1,0:T(8,128)S(1)}, f32[19,1,8,128]{3,2,1,0:T(8,128)S(1)}, u32[]{:S(2)}, u32[]{:S(2)}) collective-permute-start(f32[19,1,8,128]{3,2,1,0:T(8,128)S(1)} %get-tuple-element.297), channel_id=1, source_target_pairs={{8,0},{16,8},{24,16},{32,24},{40,32},{48,40},{56,48},{64,56},{72,6... | collective-permute-start | bytes 233480 | tf_op jit(solution)/shard_map/ppermute | solution.py:46
  57.3 9.8 %collective-permute-start.5 = (f32[19,1,8,128]{3,2,1,0:T(8,128)S(1)}, f32[19,1,8,128]{3,2,1,0:T(8,128)S(1)}, u32[]{:S(2)}, u32[]{:S(2)}) collective-permute-start(f32[19,1,8,128]{3,2,1,0:T(8,128)S(1)} %get-tuple-element.298), channel_id=1, source_target_pairs={{0,8},{8,16},{16,24},{24,32},{32,40},{40,48},{48,56},{56,64},{64,7... | collective-permute-start | bytes 233480 | tf_op jit(solution)/shard_map/ppermute | solution.py:44
  67.1 6.1 %collective-permute-start.7 = (f32[19,6,1,128]{3,2,1,0:T(1,128)S(1)}, f32[19,6,1,128]{3,2,1,0:T(1,128)S(1)}, u32[]{:S(2)}, u32[]{:S(2)}) collective-permute-start(f32[19,6,1,128]{3,2,1,0:T(1,128)S(1)} %get-tuple-element.267), channel_id=1, source_target_pairs={{0,1},{1,2},{2,3},{3,4},{4,5},{5,6},{6,7},{7,0},{8,9},{9,10},{10,1... | collective-permute-start | bytes 175112 | tf_op jit(solution)/shard_map/ppermute | solution.py:44
  69.1 12.1 %collective-permute-start.6 = (f32[19,6,1,128]{3,2,1,0:T(1,128)S(1)}, f32[19,6,1,128]{3,2,1,0:T(1,128)S(1)}, u32[]{:S(2)}, u32[]{:S(2)}) collective-permute-start(f32[19,6,1,128]{3,2,1,0:T(1,128)S(1)} %get-tuple-element.266), channel_id=1, source_target_pairs={{1,0},{2,1},{3,2},{4,3},{5,4},{6,5},{7,6},{0,7},{9,8},{10,9},{11,1... | collective-permute-start | bytes 175112 | tf_op jit(solution)/shard_map/ppermute | solution.py:46
  83.4 5.2 %collective-permute-start.8 = (f32[19,1,8,128]{3,2,1,0:T(8,128)S(1)}, f32[19,1,8,128]{3,2,1,0:T(8,128)S(1)}, u32[]{:S(2)}, u32[]{:S(2)}) collective-permute-start(f32[19,1,8,128]{3,2,1,0:T(8,128)S(1)} %get-tuple-element.293), channel_id=1, source_target_pairs={{8,0},{16,8},{24,16},{32,24},{40,32},{48,40},{56,48},{64,56},{72,6... | collective-permute-start | bytes 233480 | tf_op jit(solution)/shard_map/ppermute | solution.py:46
  85.4 9.6 %collective-permute-start.9 = (f32[19,1,8,128]{3,2,1,0:T(8,128)S(1)}, f32[19,1,8,128]{3,2,1,0:T(8,128)S(1)}, u32[]{:S(2)}, u32[]{:S(2)}) collective-permute-start(f32[19,1,8,128]{3,2,1,0:T(8,128)S(1)} %get-tuple-element.294), channel_id=1, source_target_pairs={{0,8},{8,16},{16,24},{24,32},{32,40},{40,48},{48,56},{56,64},{64,7... | collective-permute-start | bytes 233480 | tf_op jit(solution)/shard_map/ppermute | solution.py:44
  95.1 6.1 %collective-permute-start.11 = (f32[19,6,1,128]{3,2,1,0:T(1,128)S(1)}, f32[19,6,1,128]{3,2,1,0:T(1,128)S(1)}, u32[]{:S(2)}, u32[]{:S(2)}) collective-permute-start(f32[19,6,1,128]{3,2,1,0:T(1,128)S(1)} %get-tuple-element.265), channel_id=1, source_target_pairs={{0,1},{1,2},{2,3},{3,4},{4,5},{5,6},{6,7},{7,0},{8,9},{9,10},{10,1... | collective-permute-start | bytes 175112 | tf_op jit(solution)/shard_map/ppermute | solution.py:44
  97.0 12.1 %collective-permute-start.10 = (f32[19,6,1,128]{3,2,1,0:T(1,128)S(1)}, f32[19,6,1,128]{3,2,1,0:T(1,128)S(1)}, u32[]{:S(2)}, u32[]{:S(2)}) collective-permute-start(f32[19,6,1,128]{3,2,1,0:T(1,128)S(1)} %get-tuple-element.264), channel_id=1, source_target_pairs={{1,0},{2,1},{3,2},{4,3},{5,4},{6,5},{7,6},{0,7},{9,8},{10,9},{11,1... | collective-permute-start | bytes 175112 | tf_op jit(solution)/shard_map/ppermute | solution.py:46
  101.2 9.5 %copy-start.21 = (f32[1,4,8,128]{3,2,1,0:T(8,128)}, f32[1,4,8,128]{3,2,1,0:T(8,128)S(1)}, u32[]{:S(2)}) copy-start(f32[1,4,8,128]{3,2,1,0:T(8,128)S(1)} %get-tuple-element.145) | copy-start | bytes 49156
  109.1 1.6 copy-start.23
  109.2 1.5 copy-start.25
  110.1 0.7 copy-start.9
  110.2 0.6 copy-start.7
  110.3 0.6 copy-start.13
  110.3 0.6 copy-start.11
  110.4 0.6 copy-start.15
  110.6 0.6 copy-start.17
  133.5 0.8 copy-start.1
  134.3 0.8 copy-start.2
  135.2 0.8 copy-start.3
  136.0 0.8 copy-start.4
  136.9 0.8 copy-start.5
  137.7 0.8 copy-start.6
  139.2 0.7 copy-start.24
  139.2 0.7 copy-start.22
  139.2 0.8 copy-start.26
  139.2 0.8 copy-start.27
  139.9 0.7 copy-start.12
  140.0 0.7 copy-start.14
  140.0 0.7 copy-start.16
  140.0 0.8 copy-start.18
  140.0 0.7 copy-start.8
  140.0 0.7 copy-start.10
  141.7 13.0 %all-to-all-start = ((f32[2,6,1,2,32]{1,3,2,0,4:T(2,128)}), f32[2,6,1,2,32]{1,3,2,0,4:T(2,128)S(1)}, u32[]{:S(2)}, u32[]{:S(2)}) async-start(f32[2,6,1,2,32]{1,3,2,0,4:T(2,128)} %copy.521), calls=%async_computation | async-start | bytes 131072 | tf_op jit(solution)/shard_map/all_to_all | solution.py:140
  155.6 7.8 %copy-start.38 = (f32[19]{0:T(128)S(1)}, f32[19]{0:T(128)}, u32[]{:S(2)}) copy-start(f32[19]{0:T(128)} %constant.177.clone) | copy-start | bytes 232
  157.8 5.7 %copy-start.20 = (f32[4,8,128]{2,1,0:T(8,128)S(1)}, f32[4,8,128]{2,1,0:T(8,128)}, u32[]{:S(2)}) copy-start(f32[4,8,128]{2,1,0:T(8,128)} %copy-done.19) | copy-start | bytes 49156
  157.8 15.5 %all-to-all-start.1 = ((f32[2,6,1,64]{1,0,2,3:T(2,128)}), f32[2,6,1,64]{1,0,2,3:T(2,128)S(1)}, u32[]{:S(2)}, u32[]{:S(2)}) async-start(f32[2,6,1,64]{1,0,2,3:T(2,128)} %copy.529), calls=%async_computation.1 | async-start | bytes 131072 | tf_op jit(solution)/shard_map/all_to_all | solution.py:145
  163.4 0.7 copy-start.31
  163.4 0.7 copy-start.33
  163.4 0.7 copy-start.36
  213.8 14.6 %all-to-all-start.2 = ((f32[64,2,3,1,1]{2,1,4,3,0:T(2,128)}), f32[64,2,3,1,1]{2,1,4,3,0:T(2,128)S(1)}, u32[]{:S(2)}, u32[]{:S(2)}) async-start(f32[64,2,3,1,1]{2,1,4,3,0:T(2,128)} %constant_dynamic-update-slice_fusion.176), calls=%async_computation.2 | async-start | bytes 131072 | tf_op jit(solution)/shard_map/all_to_all | solution.py:197
  230.3 13.5 %all-to-all-start.3 = ((f32[2,3,1,16,4]{4,0,2,1,3:T(2,128)}), f32[2,3,1,16,4]{4,0,2,1,3:T(2,128)S(1)}, u32[]{:S(2)}, u32[]{:S(2)}) async-start(f32[2,3,1,16,4]{4,0,2,1,3:T(2,128)} %copy.536), calls=%async_computation.3 | async-start | bytes 98304 | tf_op jit(solution)/shard_map/all_to_all | solution.py:204
  235.7 9.4 %collective-permute-start.13 = (f32[19,1,8,128]{3,2,1,0:T(8,128)S(1)}, f32[19,1,8,128]{3,2,1,0:T(8,128)S(1)}, u32[]{:S(2)}, u32[]{:S(2)}) collective-permute-start(f32[19,1,8,128]{3,2,1,0:T(8,128)S(1)} %get-tuple-element.289), channel_id=1, source_target_pairs={{8,0},{16,8},{24,16},{32,24},{40,32},{48,40},{56,48},{64,56},{72,6... | collective-permute-start | bytes 233480 | tf_op jit(solution)/shard_map/ppermute | solution.py:46
  238.0 9.6 %collective-permute-start.12 = (f32[19,1,8,128]{3,2,1,0:T(8,128)S(1)}, f32[19,1,8,128]{3,2,1,0:T(8,128)S(1)}, u32[]{:S(2)}, u32[]{:S(2)}) collective-permute-start(f32[19,1,8,128]{3,2,1,0:T(8,128)S(1)} %get-tuple-element.290), channel_id=1, source_target_pairs={{0,8},{8,16},{16,24},{24,32},{32,40},{40,48},{48,56},{56,64},{64,7... | collective-permute-start | bytes 233480 | tf_op jit(solution)/shard_map/ppermute | solution.py:44
  247.7 9.2 %collective-permute-start.14 = (f32[19,6,1,128]{3,2,1,0:T(1,128)S(1)}, f32[19,6,1,128]{3,2,1,0:T(1,128)S(1)}, u32[]{:S(2)}, u32[]{:S(2)}) collective-permute-start(f32[19,6,1,128]{3,2,1,0:T(1,128)S(1)} %get-tuple-element.263), channel_id=1, source_target_pairs={{0,1},{1,2},{2,3},{3,4},{4,5},{5,6},{6,7},{7,0},{8,9},{9,10},{10,1... | collective-permute-start | bytes 175112 | tf_op jit(solution)/shard_map/ppermute | solution.py:44
  255.0 12.1 %collective-permute-start.15 = (f32[19,6,1,128]{3,2,1,0:T(1,128)S(1)}, f32[19,6,1,128]{3,2,1,0:T(1,128)S(1)}, u32[]{:S(2)}, u32[]{:S(2)}) collective-permute-start(f32[19,6,1,128]{3,2,1,0:T(1,128)S(1)} %get-tuple-element.262), channel_id=1, source_target_pairs={{1,0},{2,1},{3,2},{4,3},{5,4},{6,5},{7,6},{0,7},{9,8},{10,9},{11,1... | collective-permute-start | bytes 175112 | tf_op jit(solution)/shard_map/ppermute | solution.py:46
